TPU v7x, 32 devices: a whole 2x2x4 slice. The times are simulated.
32 devices in a mesh: batch: 2 (over x), head: 2 (over core), expert: 8 (over z, y).
Axes of the slice: x: 2, y: 2, z: 4, core: 2. Of those that a mesh axis runs over, the one named last changes fastest.
Arguments:
- hidden_in: bfloat16 [4096, 2048], P(('batch', 'head', 'expert')), may hold values from -6 to 6
- norm_gain: float32 [2048], replicated, may hold values from 0.25 to 1.75
- w_gate: bfloat16 [16, 2048, 384], P('expert', ('batch', 'head')), may hold values from -0.125 to 0.125
- w_up: bfloat16 [16, 2048, 384], P('expert', ('batch', 'head')), may hold values from -0.125 to 0.125
- w_down: bfloat16 [16, 384, 2048], P('expert', None, ('batch', 'head')), may hold values from -0.3125 to 0.3125
- expert_ids: int32 [4096, 2], P(('batch', 'head', 'expert')), may hold values from 0 to 15, all different within a row; in each aligned block of 128 rows (0 to 127, 128 to 255, ...) at most 24 rows name the same one
- gate_codes: int32 [4096, 2], P(('batch', 'head', 'expert')), may hold values from 4096 to 65535
- out_grad: bfloat16 [4096, 2048], P(('batch', 'head', 'expert')), may hold values from -6 to 6
Outputs:
- output: bfloat16 [4096, 2048], P(('batch', 'head', 'expert'))
- grad_in: bfloat16 [4096, 2048], P(('batch', 'head', 'expert'))
Inputs may be any that keep to these rules, and one draw needn't show every extreme that they name: `expert_ids`: each row names 2 different experts; within the rows of one device no expert is named more than 24 times, a bound that some block reaches.
All inputs are finite; a program needn't handle non-finite values.
Results may differ from a plain program's by a relative error of at most 0.0055.
Values may be sent and summed in bfloat16 or wider, within the bound.
A program may use at most 128 MiB of HBM per device.

v0:
```python
import jax
import jax.numpy as jnp
from jax import lax
from jax.sharding import PartitionSpec as P

epsilon = 1e-06


def slot_tables(expert_ids, expert_total, capacity):
    chosen = expert_ids.shape[1]
    routes = expert_ids.reshape(-1)
    route_total = routes.shape[0]
    labels = jnp.arange(expert_total, dtype=jnp.int32)
    onehot = (routes[:, None] == labels[None, :]).astype(jnp.int32)
    before = jnp.cumsum(onehot, axis=0) - onehot
    position = jnp.sum(before * onehot, axis=1)
    slot_ids = routes * capacity + position
    owner_rows = jnp.arange(route_total, dtype=jnp.int32) // chosen
    source_rows = jnp.zeros((expert_total * capacity,), jnp.int32).at[slot_ids].set(owner_rows)
    filled = jnp.zeros((expert_total * capacity,), jnp.int32).at[slot_ids].set(1)
    return (slot_ids, source_rows, filled)


def expert_forward(slot_rows, gate_mat, up_mat, down_mat):
    gate_pre = jnp.dot(slot_rows, gate_mat, preferred_element_type=jnp.float32)
    up_pre = jnp.dot(slot_rows, up_mat, preferred_element_type=jnp.float32)
    inner_rows = (jax.nn.silu(gate_pre) * up_pre).astype(jnp.bfloat16)
    result = jnp.dot(inner_rows, down_mat, preferred_element_type=jnp.float32).astype(jnp.bfloat16)
    return (result, gate_pre, up_pre)


def expert_backward(slot_grads, gate_pre, up_pre, gate_mat, up_mat, down_mat):
    back_grad = jnp.dot(slot_grads, down_mat.T, preferred_element_type=jnp.float32)
    sigmoid_gate = jax.nn.sigmoid(gate_pre)
    grad_gate = (
        back_grad * up_pre * sigmoid_gate * (1.0 + gate_pre * (1.0 - sigmoid_gate))
    ).astype(jnp.bfloat16)
    grad_up = (back_grad * jax.nn.silu(gate_pre)).astype(jnp.bfloat16)
    grad_rows = jnp.dot(grad_gate, gate_mat.T, preferred_element_type=jnp.float32)
    grad_rows = grad_rows + jnp.dot(grad_up, up_mat.T, preferred_element_type=jnp.float32)
    return grad_rows.astype(jnp.bfloat16)


def body(hidden_in, norm_gain, w_gate, w_up, w_down, expert_ids, gate_codes, out_grad):
    owners = lax.axis_size("expert")
    local_count = w_gate.shape[0]
    expert_total = owners * local_count
    tok_rows, features = hidden_in.shape
    chosen = expert_ids.shape[1]
    capacity = 3 * tok_rows * chosen // (2 * expert_total)
    hidden_float = hidden_in.astype(jnp.float32)
    row_scale = lax.rsqrt(jnp.mean(hidden_float * hidden_float, axis=1, keepdims=True) + epsilon)
    normed = (hidden_float * row_scale * norm_gain).astype(jnp.bfloat16)
    code_values = gate_codes.astype(jnp.float32)
    weights = code_values / jnp.sum(code_values, axis=1, keepdims=True)
    slot_ids, source_rows, filled = slot_tables(expert_ids, expert_total, capacity)
    order_rows = source_rows.reshape(owners, local_count, capacity).transpose(1, 0, 2).reshape(-1)
    order_live = filled.reshape(owners, local_count, capacity).transpose(1, 0, 2).reshape(-1)
    keep = (order_live == 1)[:, None]
    nothing = jnp.zeros((), jnp.bfloat16)
    slot_shape = (local_count, owners, capacity, features)
    flat_shape = (local_count, owners * capacity, features)
    send_normed = jnp.where(keep, normed[order_rows], nothing).reshape(slot_shape)
    send_grad = jnp.where(keep, out_grad[order_rows], nothing).reshape(slot_shape)
    gate_full, up_full, down_full = (
        lax.all_gather(w_gate, ("batch", "head"), axis=1, tiled=True),
        lax.all_gather(w_up, ("batch", "head"), axis=1, tiled=True),
        lax.all_gather(w_down, ("batch", "head"), axis=2, tiled=True),
    )
    forward = jax.vmap(expert_forward)
    backward = jax.vmap(expert_backward)
    arrived = lax.all_to_all(send_normed, "expert", split_axis=1, concat_axis=1, tiled=True)
    result, gate_pre, up_pre = forward(arrived.reshape(flat_shape), gate_full, up_full, down_full)
    returned = lax.all_to_all(
        result.reshape(slot_shape), "expert", split_axis=1, concat_axis=1, tiled=True
    )
    arrived_grad = lax.all_to_all(send_grad, "expert", split_axis=1, concat_axis=1, tiled=True)
    grad_rows = backward(
        arrived_grad.reshape(flat_shape), gate_pre, up_pre, gate_full, up_full, down_full
    )
    returned_grad = lax.all_to_all(
        grad_rows.reshape(slot_shape), "expert", split_axis=1, concat_axis=1, tiled=True
    )
    expert_of = slot_ids // capacity
    position = slot_ids % capacity
    flat_index = (expert_of % local_count * owners + expert_of // local_count) * capacity + position
    picked = (
        returned.reshape(-1, features)[flat_index]
        .astype(jnp.float32)
        .reshape(tok_rows, chosen, features)
    )
    mixture = jnp.sum(picked * weights[:, :, None], axis=1)
    output = (hidden_float + mixture).astype(jnp.bfloat16)
    picked_grad = (
        returned_grad.reshape(-1, features)[flat_index]
        .astype(jnp.float32)
        .reshape(tok_rows, chosen, features)
    )
    grad_normed = jnp.sum(picked_grad * weights[:, :, None], axis=1)
    scaled = norm_gain * grad_normed
    inner_mean = jnp.mean(scaled * hidden_float, axis=1, keepdims=True)
    grad_in = (
        out_grad.astype(jnp.float32)
        + row_scale * scaled
        - hidden_float * (row_scale * row_scale * row_scale) * inner_mean
    )
    return (output, grad_in.astype(jnp.bfloat16))


def solution(mesh):
    in_specs = (
        P(("batch", "head", "expert"), None),
        P(),
        P("expert", ("batch", "head"), None),
        P("expert", ("batch", "head"), None),
        P("expert", None, ("batch", "head")),
        P(("batch", "head", "expert"), None),
        P(("batch", "head", "expert"), None),
        P(("batch", "head", "expert"), None),
    )
    out_specs = (P(("batch", "head", "expert"), None), P(("batch", "head", "expert"), None))
    return jax.shard_map(body, mesh=mesh, in_specs=in_specs, out_specs=out_specs, check_vma=False)
```

profile of v0, /device:TPU:30, one launch (start us, length us, event | category | flops | bytes accessed | tf_op | source)
XLA Modules:
  0.0 229.4 jit_solution(799432135210775222)
XLA Ops:
  7.2 0.7 all-gather.4.cloned.1.call-update
  8.0 0.7 all-gather.6.cloned.1.call-update
  8.7 0.1 copy.25
  8.8 0.1 eq.48
  8.9 0.1 eq.44
  9.1 0.6 reduce-window.6
  9.7 0.2 slice_reduce_fusion
  9.9 0.1 copy.24
  10.0 0.1 mul.147
  10.3 1.4 scatter_custom_fusion.1
  12.0 0.2 fusion
  12.2 0.2 fusion.2
  12.4 2.5 %gather_fusion = bf16[384,2048]{1,0:T(8,128)(2,1)S(1)} fusion(bf16[128,2048]{1,0:T(8,128)(2,1)S(1)} %fusion.2, s32[1024]{0:T(1024)S(1)} %pad_clamp_fusion.1), kind=kCustom, calls=%fused_computation | custom fusion | bytes 3147264 | tf_op jit(solution)/shard_map/gather | solution.py:63
  14.9 3.1 %gather_fusion.2 = bf16[384,2048]{1,0:T(8,128)(2,1)} fusion(bf16[128,2048]{1,0:T(8,128)(2,1)S(1)} %copy-done, s32[1024]{0:T(1024)S(1)} %pad_clamp_fusion.1), kind=kCustom, calls=%fused_computation.2 | custom fusion | bytes 3147264 | tf_op jit(solution)/shard_map/gather | solution.py:64
  18.0 1.4 scatter_custom_fusion
  19.5 3.4 %copy_select_fusion = (bf16[2,8,24,2048]{3,2,0,1:T(8,128)(2,1)}, bf16[2,8,24,2048]{3,2,0,1:T(8,128)(2,1)}) fusion(bf16[2,8,24,2048]{3,2,1,0:T(8,128)(2,1)} %bitcast.48, pred[2,8,24]{2,0,1:T(4,128)(4,1)S(1)} %bitcast.51, bf16[2,8,24,2048]{3,2,1,0:T(8,128)(2,1)S(1)} %bitcast.47), kind=kLoop, calls=%fused_computation.15 | loop fusion | flops 1572864 | bytes 6291840 | tf_op jit(solution)/shard_map/jit(_where)/select_n | solution.py:64
  22.8 6.0 %all-to-all-start = ((bf16[2,8,24,2048]{3,2,0,1:T(8,128)(2,1)}), bf16[2,8,24,2048]{3,2,0,1:T(8,128)(2,1)S(1)}, u32[]{:S(2)}, u32[]{:S(2)}) async-start(bf16[2,8,24,2048]{3,2,0,1:T(8,128)(2,1)} %get-tuple-element.7), calls=%async_computation | async-start | bytes 3145728 | tf_op jit(solution)/shard_map/all_to_all | solution.py:72
  28.8 0.7 all-gather.8.cloned.1.call-update
  29.5 34.0 %all-to-all-done = bf16[2,8,24,2048]{3,2,0,1:T(8,128)(2,1)S(1)} async-done(((bf16[2,8,24,2048]{3,2,0,1:T(8,128)(2,1)}), bf16[2,8,24,2048]{3,2,0,1:T(8,128)(2,1)S(1)}, u32[]{:S(2)}, u32[]{:S(2)}) %all-to-all-start) | async-done | bytes 1572896 | tf_op jit(solution)/shard_map/all_to_all | solution.py:72
  63.6 1.2 copy-done.6
  64.8 6.6 %all-to-all-start.2 = ((bf16[2,8,24,2048]{3,2,0,1:T(8,128)(2,1)}), bf16[2,8,24,2048]{3,2,0,1:T(8,128)(2,1)}, u32[]{:S(2)}, u32[]{:S(2)}) async-start(bf16[2,8,24,2048]{3,2,0,1:T(8,128)(2,1)} %get-tuple-element.6), calls=%async_computation.2 | async-start | bytes 3145728 | tf_op jit(solution)/shard_map/all_to_all | solution.py:77
  71.4 1.5 copy.30
  72.9 32.8 %all-to-all-done.2 = bf16[2,8,24,2048]{3,2,0,1:T(8,128)(2,1)} async-done(((bf16[2,8,24,2048]{3,2,0,1:T(8,128)(2,1)}), bf16[2,8,24,2048]{3,2,0,1:T(8,128)(2,1)}, u32[]{:S(2)}, u32[]{:S(2)}) %all-to-all-start.2) | async-done | bytes 1572896 | tf_op jit(solution)/shard_map/all_to_all | solution.py:77
  105.7 2.8 %copy.35 = bf16[2,8,24,2048]{3,2,1,0:T(8,128)(2,1)} copy(bf16[2,8,24,2048]{3,2,0,1:T(8,128)(2,1)} %all-to-all-done.2) | data formatting | bytes 3145728 | tf_op jit(solution)/shard_map/all_to_all | solution.py:77
  108.5 2.9 %fusion.28 = f32[2,192,384]{2,1,0:T(8,128)S(1)} fusion(bf16[2,192,2048]{2,1,0:T(8,128)(2,1)S(1)} %bitcast.43, bf16[2,2048,384]{2,1,0:T(8,128)(2,1)} %all-gather.4.cloned.1.call-done), kind=kOutput, calls=%fused_computation.75 | convolution fusion | flops 603979776 | bytes 5308416 | tf_op jit(solution)/shard_map/vmap()/dot_general | solution.py:25
  111.4 3.7 %fusion.29 = f32[2,192,384]{2,1,0:T(8,128)} fusion(bf16[2,192,2048]{2,1,0:T(8,128)(2,1)S(1)} %bitcast.44, bf16[2,2048,384]{2,1,0:T(8,128)(2,1)} %all-gather.6.cloned.1.call-done), kind=kOutput, calls=%fused_computation.76 | convolution fusion | flops 603979776 | bytes 5308416 | tf_op jit(solution)/shard_map/vmap()/dot_general | solution.py:26
  115.1 3.7 %fusion.30 = f32[2,192,384]{2,1,0:T(8,128)S(1)} fusion(bf16[2,192,2048]{2,1,0:T(8,128)(2,1)} %bitcast.45, bf16[2,384,2048]{2,1,0:T(8,128)(2,1)} %all-gather.8.cloned.1.call-done), kind=kOutput, calls=%fused_computation.77 | convolution fusion | flops 603979776 | bytes 5308416 | tf_op jit(solution)/shard_map/vmap()/dot_general | solution.py:33
  118.8 1.3 fusion.9
  120.1 0.6 copy-done.1
  120.6 1.3 add_convert_fusion
  121.9 1.3 copy.36
  123.2 6.0 %all-to-all-start.3 = ((bf16[2,8,24,2048]{3,2,0,1:T(8,128)(2,1)}), bf16[2,8,24,2048]{3,2,0,1:T(8,128)(2,1)S(1)}, u32[]{:S(2)}, u32[]{:S(2)}) async-start(bf16[2,8,24,2048]{3,2,0,1:T(8,128)(2,1)} %copy.36), calls=%async_computation.3 | async-start | bytes 3145728 | tf_op jit(solution)/shard_map/all_to_all | solution.py:81
  129.2 3.1 %convolution_convert_fusion = bf16[2,192,2048]{2,1,0:T(8,128)(2,1)S(1)} fusion(bf16[2,384,2048]{2,1,0:T(8,128)(2,1)} %all-gather.8.cloned.1.call-done, f32[2,192,384]{2,1,0:T(8,128)} %fusion.29, f32[2,192,384]{2,1,0:T(8,128)S(1)} %fusion.28), kind=kOutput, calls=%fused_computation.7 | convolution fusion | flops 605650944 | bytes 5898240 | tf_op jit(solution)/shard_map/vmap()/dot_general | solution.py:28
  132.3 1.3 copy.31
  133.5 30.5 %all-to-all-done.3 = bf16[2,8,24,2048]{3,2,0,1:T(8,128)(2,1)S(1)} async-done(((bf16[2,8,24,2048]{3,2,0,1:T(8,128)(2,1)}), bf16[2,8,24,2048]{3,2,0,1:T(8,128)(2,1)S(1)}, u32[]{:S(2)}, u32[]{:S(2)}) %all-to-all-start.3) | async-done | bytes 1572896 | tf_op jit(solution)/shard_map/all_to_all | solution.py:81
  164.0 1.2 copy-done.5
  165.2 6.8 %all-to-all-start.1 = ((bf16[2,8,24,2048]{3,2,0,1:T(8,128)(2,1)}), bf16[2,8,24,2048]{3,2,0,1:T(8,128)(2,1)}, u32[]{:S(2)}, u32[]{:S(2)}) async-start(bf16[2,8,24,2048]{3,2,0,1:T(8,128)(2,1)} %copy.31), calls=%async_computation.1 | async-start | bytes 3145728 | tf_op jit(solution)/shard_map/all_to_all | solution.py:74
  172.0 0.1 copy.33
  172.1 1.5 copy.37
  173.6 2.4 %gather_fusion.3 = bf16[256,2048]{1,0:T(8,128)(2,1)} fusion(bf16[384,2048]{1,0:T(8,128)(2,1)S(1)} %bitcast.42, s32[1024]{0:T(1024)S(1)} %pad_clamp_fusion), kind=kCustom, calls=%fused_computation.3 | custom fusion | bytes 2098176 | tf_op jit(solution)/shard_map/gather | solution.py:95
  176.0 3.4 %reshape.292 = f32[128,2,2048]{2,1,0:T(2,128)} reshape(bf16[256,2048]{1,0:T(8,128)(2,1)} %gather_fusion.3) | data formatting | bytes 3145728 | tf_op jit(solution)/shard_map/convert_element_type | solution.py:96
  179.4 26.7 %all-to-all-done.1 = bf16[2,8,24,2048]{3,2,0,1:T(8,128)(2,1)} async-done(((bf16[2,8,24,2048]{3,2,0,1:T(8,128)(2,1)}), bf16[2,8,24,2048]{3,2,0,1:T(8,128)(2,1)}, u32[]{:S(2)}, u32[]{:S(2)}) %all-to-all-start.1) | async-done | bytes 1572896 | tf_op jit(solution)/shard_map/all_to_all | solution.py:74
  206.1 1.5 copy.32
  207.6 2.3 %gather_fusion.1 = bf16[256,2048]{1,0:T(8,128)(2,1)} fusion(bf16[384,2048]{1,0:T(8,128)(2,1)S(1)} %bitcast.41, s32[1024]{0:T(1024)S(1)} %pad_clamp_fusion), kind=kCustom, calls=%fused_computation.1 | custom fusion | bytes 2098176 | tf_op jit(solution)/shard_map/gather | solution.py:88
  210.0 3.5 %reshape.291 = f32[128,2,2048]{2,1,0:T(2,128)} reshape(bf16[256,2048]{1,0:T(8,128)(2,1)} %gather_fusion.1) | data formatting | bytes 3145728 | tf_op jit(solution)/shard_map/convert_element_type | solution.py:89
  213.4 7.7 %multiply_reduce_fusion = (f32[128,2048]{1,0:T(8,128)S(1)}, f32[128,2048]{1,0:T(8,128)S(1)}) fusion(f32[128,2,2048]{2,1,0:T(2,128)S(1)} %copy-done.3, f32[128,2]{1,0:T(8,128)S(1)} %copy.33, f32[128,2,2048]{2,1,0:T(2,128)} %reshape.291), kind=kLoop, calls=%fused_computation.8 | loop fusion | flops 1572864 | bytes 6292480 | tf_op jit(solution)/shard_map/reduce_sum | solution.py:99
  221.2 0.2 fusion.7
  221.4 1.4 fusion.6
  (45 shorter events, 0.7 us)
Async XLA Ops:
  7.2 1.5 copy-start.9
  7.2 4.8 %copy-start.4 = (bf16[128,2048]{1,0:T(8,128)(2,1)S(1)}, bf16[128,2048]{1,0:T(8,128)(2,1)}, u32[]{:S(2)}) copy-start(bf16[128,2048]{1,0:T(8,128)(2,1)} %param.8) | copy-start | bytes 1572868
  7.2 5.0 %copy-start.8 = (f32[2048]{0:T(1024)S(1)}, f32[2048]{0:T(1024)}, u32[]{:S(2)}) copy-start(f32[2048]{0:T(1024)} %param.9) | copy-start | bytes 24580
  7.2 101.3 %all-gather.4.cloned.1.call-start = ((), (), s32[]{:S(2)}) async-start(), calls=%async_computation.4 | async-start | bytes 3932160 | tf_op jit(solution)/shard_map/all_gather | solution.py:66
  7.9 103.4 %all-gather.6.cloned.1.call-start = ((), (), s32[]{:S(2)}) async-start(), calls=%async_computation.5 | async-start | bytes 3932160 | tf_op jit(solution)/shard_map/all_gather | solution.py:67
  12.4 2.5 %copy-start = (bf16[128,2048]{1,0:T(8,128)(2,1)S(1)}, bf16[128,2048]{1,0:T(8,128)(2,1)}, u32[]{:S(2)}) copy-start(bf16[128,2048]{1,0:T(8,128)(2,1)} %param.15) | copy-start | bytes 1572868
  22.8 40.7 %all-to-all-start = ((bf16[2,8,24,2048]{3,2,0,1:T(8,128)(2,1)}), bf16[2,8,24,2048]{3,2,0,1:T(8,128)(2,1)S(1)}, u32[]{:S(2)}, u32[]{:S(2)}) async-start(bf16[2,8,24,2048]{3,2,0,1:T(8,128)(2,1)} %get-tuple-element.7), calls=%async_computation | async-start | bytes 3145728 | tf_op jit(solution)/shard_map/all_to_all | solution.py:72
  28.8 86.2 %all-gather.8.cloned.1.call-start = ((), (), s32[]{:S(2)}) async-start(), calls=%async_computation.6 | async-start | bytes 3932160 | tf_op jit(solution)/shard_map/all_gather | solution.py:68
  63.6 1.2 copy-start.6
  64.8 40.9 %all-to-all-start.2 = ((bf16[2,8,24,2048]{3,2,0,1:T(8,128)(2,1)}), bf16[2,8,24,2048]{3,2,0,1:T(8,128)(2,1)}, u32[]{:S(2)}, u32[]{:S(2)}) async-start(bf16[2,8,24,2048]{3,2,0,1:T(8,128)(2,1)} %get-tuple-element.6), calls=%async_computation.2 | async-start | bytes 3145728 | tf_op jit(solution)/shard_map/all_to_all | solution.py:77
  115.1 3.7 %copy-start.2 = (bf16[2,2048,384]{2,1,0:T(8,128)(2,1)S(1)}, bf16[2,2048,384]{2,1,0:T(8,128)(2,1)}, u32[]{:S(2)}) copy-start(bf16[2,2048,384]{2,1,0:T(8,128)(2,1)} %all-gather.4.cloned.1.call-done) | copy-start | bytes 9437188
  115.1 3.7 %copy-start.7 = (f32[2,192,384]{2,1,0:T(8,128)S(1)}, f32[2,192,384]{2,1,0:T(8,128)}, u32[]{:S(2)}) copy-start(f32[2,192,384]{2,1,0:T(8,128)} %fusion.29) | copy-start | bytes 1769476
  118.8 1.9 copy-start.1
  123.2 40.8 %all-to-all-start.3 = ((bf16[2,8,24,2048]{3,2,0,1:T(8,128)(2,1)}), bf16[2,8,24,2048]{3,2,0,1:T(8,128)(2,1)S(1)}, u32[]{:S(2)}, u32[]{:S(2)}) async-start(bf16[2,8,24,2048]{3,2,0,1:T(8,128)(2,1)} %copy.36), calls=%async_computation.3 | async-start | bytes 3145728 | tf_op jit(solution)/shard_map/all_to_all | solution.py:81
  133.5 38.4 %copy-start.10 = (s32[128,2]{0,1:T(2,128)S(1)}, s32[128,2]{0,1:T(2,128)}, u32[]{:S(2)}) copy-start(s32[128,2]{0,1:T(2,128)} %param.14) | copy-start | bytes 3076
  164.0 1.2 copy-start.5
  165.2 40.9 %all-to-all-start.1 = ((bf16[2,8,24,2048]{3,2,0,1:T(8,128)(2,1)}), bf16[2,8,24,2048]{3,2,0,1:T(8,128)(2,1)}, u32[]{:S(2)}, u32[]{:S(2)}) async-start(bf16[2,8,24,2048]{3,2,0,1:T(8,128)(2,1)} %copy.31), calls=%async_computation.1 | async-start | bytes 3145728 | tf_op jit(solution)/shard_map/all_to_all | solution.py:74
  209.9 3.5 %copy-start.3 = (f32[128,2,2048]{2,1,0:T(2,128)S(1)}, f32[128,2,2048]{2,1,0:T(2,128)}, u32[]{:S(2)}) copy-start(f32[128,2,2048]{2,1,0:T(2,128)} %reshape.292) | copy-start | bytes 6291460
Sparse Core Ops, SparseCore 0:
  9.6 28.4 all-gather.3
  39.7 28.4 all-gather.5
  69.8 28.4 all-gather.7
where the time goes:
time: 234 us; the launch traced here: 229 us
  waiting for transfers between devices  126 us (54%)
  local copies, waits for them, and re-layouts  33.9 us (14%)
  starting transfers between devices  25.4 us (11%)
  matrix products  15.9 us (7%)
  other arithmetic  14 us (6%)
  between operations  14 us (6%)
    all_to_all x1, waiting for transfers between devices, body(): lax.all_to_all(send_normed, 'expert', split_axis=1, concat_axis=1, tiled=...  34 us
    all_to_all x1, waiting for transfers between devices, body(): lax.all_to_all(send_grad, 'expert', split_axis=1, concat_axis=1, tiled=True)  32.8 us
    all_to_all x1, waiting for transfers between devices, body(): lax.all_to_all(grad_rows.reshape(slot_shape), 'expert', split_axis=1, con...  30.5 us
    all_to_all x1, waiting for transfers between devices, body(): lax.all_to_all(result.reshape(slot_shape), 'expert', split_axis=1, concat...  26.7 us
    reduce_sum x1, other arithmetic, body(): grad_normed = jnp.sum(picked_grad * weights[:, :, None], axis=1)  7.73 us
    all_to_all x1, starting transfers between devices, body(): lax.all_to_all(result.reshape(slot_shape), 'expert', split_axis=1, concat...  6.77 us
    all_to_all x1, starting transfers between devices, body(): lax.all_to_all(send_grad, 'expert', split_axis=1, concat_axis=1, tiled=True)  6.59 us
    all_to_all x1, starting transfers between devices, body(): lax.all_to_all(grad_rows.reshape(slot_shape), 'expert', split_axis=1, con...  6 us
  transfers between devices with their start and end apart: 7, of which 4 were waited for; matrix products, arithmetic and copies ran while one was open for 16% of the time, Pallas kernels for 0%

commit v1 on v0

v1 whole, which is shorter than its diff:
```python
import functools

import jax
import jax.numpy as jnp
import numpy as np
from jax import lax
from jax.experimental import pallas as pl
from jax.experimental.pallas import tpu as pltpu
from jax.sharding import PartitionSpec as P

epsilon = 1e-06
MESH = pl.DeviceIdType.MESH
BF = jnp.bfloat16
F32 = jnp.float32
NN = (((1,), (0,)), ((), ()))
NT = (((1,), (1,)), ((), ()))
TN = (((0,), (0,)), ((), ()))


def mm(a, b, dims=NN):
    return lax.dot_general(a, b, dims, preferred_element_type=F32)


def kernel(
    sizes, hid, gain, wg_in, wu_in, wd_in, ids, codes, og, base, pick, place, out, gin,
    wg, wu, wd, send_n, send_g, recv_n, recv_g, res, gres, ret, gret, gp, up, scaled, table,
    s_sem, r_sem, own_sem, wb_send, wh_send, w_recv, w_own,
):
    n, nb, nh, cap, rows, local = sizes
    me, mb, mh = (lax.axis_index(a) for a in ("expert", "batch", "head"))
    tok, features = hid.shape
    chunks = nb * nh
    width = features // chunks
    mine = mb * nh + mh
    peers = (("expert", me, n), ("batch", mb, nb), ("head", mh, nh))

    barrier = pltpu.get_barrier_semaphore()
    for axis, at, count in peers:
        @pl.loop(1, count)
        def _(k, axis=axis, at=at, count=count):
            pl.semaphore_signal(
                barrier, inc=1, device_id={axis: lax.rem(at + k, count)}, device_id_type=MESH
            )
    pl.semaphore_wait(barrier, n + nb + nh - 3)

    tensors = ((wg_in, wg), (wu_in, wu), (wd_in, wd))

    def to_batch(i, k):
        src, dst = tensors[i]
        other = lax.rem(mb + k, nb)
        return pltpu.make_async_remote_copy(
            src_ref=src, dst_ref=dst.at[mine], send_sem=wb_send.at[i, k], recv_sem=w_recv.at[i, mine],
            device_id={"batch": other}, device_id_type=MESH,
        )

    def to_head(i, j, k):
        src, dst = tensors[i]
        b = lax.rem(mb + j, nb)
        slot = b * nh + mh
        return pltpu.make_async_remote_copy(
            src_ref=src if j == 0 else dst.at[slot], dst_ref=dst.at[slot],
            send_sem=wh_send.at[i, j, k], recv_sem=w_recv.at[i, slot],
            device_id={"head": lax.rem(mh + k, nh)}, device_id_type=MESH,
        )

    def arrived(i, slot):
        dst = tensors[i][1].at[slot]
        pltpu.make_async_copy(dst, dst, w_recv.at[i, slot]).wait()

    def keep_own(i):
        return pltpu.make_async_copy(tensors[i][0], tensors[i][1].at[mine], w_own.at[i])

    for i in range(3):
        @pl.loop(1, nb)
        def _(k, i=i):
            to_batch(i, k).start()
        keep_own(i).start()

    def block(ref, d):
        return ref.at[pl.ds(pl.multiple_of(d * rows, 16), rows)]

    def row_copy(step, src, dst, k):
        other = lax.rem(me + k, n)
        return pltpu.make_async_remote_copy(
            src_ref=block(src, other), dst_ref=block(dst, me),
            send_sem=s_sem.at[step, k], recv_sem=r_sem.at[step, k],
            device_id={"expert": other}, device_id_type=MESH,
        )

    flows = ((send_n, recv_n), (send_g, recv_g), (res, ret), (gres, gret))

    def own_copy(step):
        src, dst = flows[step]
        return pltpu.make_async_copy(block(src, me), block(dst, me), own_sem.at[step])

    def start(step):
        @pl.loop(1, n)
        def _(k):
            row_copy(step, *flows[step], k).start()
        own_copy(step).start()

    def finish(step):
        @pl.loop(1, n)
        def _(k):
            dst = block(flows[step][1], lax.rem(me + n - k, n))
            pltpu.make_async_copy(dst, dst, r_sem.at[step, k]).wait()
        own_copy(step).wait()

    def cols(c):
        return pl.ds(pl.multiple_of(c * width, 128), width)

    experts = base.shape[1]
    chosen = ids.shape[1]
    lanes = lax.broadcasted_iota(jnp.int32, (tok, experts), 1)
    hits = [(ids[:, k:k + 1] == lanes).astype(F32) for k in range(chosen)]
    total = functools.reduce(jnp.add, hits)
    earlier = (
        lax.broadcasted_iota(jnp.int32, (tok, tok), 1) < lax.broadcasted_iota(jnp.int32, (tok, tok), 0)
    ).astype(F32).astype(BF)
    where = mm(earlier, total.astype(BF)) + base[...]
    slots = lax.broadcasted_iota(jnp.int32, (tok, n * rows), 1).astype(F32)
    marks = [(slots == jnp.sum(where * h, axis=1, keepdims=True)).astype(F32) for h in hits]
    table[...] = functools.reduce(jnp.add, marks).astype(BF)

    def square(c, acc):
        v = hid[:, cols(c)].astype(F32)
        return acc + jnp.sum(v * v, axis=1, keepdims=True)

    zero = jnp.zeros((tok, 1), F32)
    scale = lax.rsqrt(lax.fori_loop(0, chunks, square, zero) / features + epsilon)

    @pl.loop(0, chunks)
    def _(c):
        v = (hid[:, cols(c)].astype(F32) * scale * gain[:, cols(c)]).astype(BF)
        send_n[:, cols(c)] = mm(table[...], v, TN).astype(BF)
    start(0)

    @pl.loop(0, chunks)
    def _(c):
        send_g[:, cols(c)] = mm(table[...], og[:, cols(c)], TN).astype(BF)
    start(1)

    for i in range(3):
        for j in range(nb):
            if j > 0:
                arrived(i, lax.rem(mb + j, nb) * nh + mh)
            for k in range(1, nh):
                to_head(i, j, k).start()
    for i in range(3):
        keep_own(i).wait()
        for b in range(nb):
            for k in range(1, nh):
                arrived(i, b * nh + lax.rem(mh + k, nh))

    finish(0)
    gp[...] = jnp.zeros_like(gp)
    up[...] = jnp.zeros_like(up)

    @pl.loop(0, chunks)
    def _(c):
        x = recv_n[:, cols(c)]
        for e in range(local):
            xe = mm(pick[e], x).astype(BF)
            gp[e] += mm(xe, wg[c, e])
            up[e] += mm(xe, wu[c, e])

    inner = [(jax.nn.silu(gp[e]) * up[e]).astype(BF) for e in range(local)]

    @pl.loop(0, chunks)
    def _(c):
        parts = [mm(place[e], mm(inner[e], wd[c, e]).astype(BF)) for e in range(local)]
        res[:, cols(c)] = functools.reduce(jnp.add, parts).astype(BF)
    start(2)

    finish(1)

    def back(c, acc):
        y = recv_g[:, cols(c)]
        return tuple(
            acc[e] + mm(mm(pick[e], y).astype(BF), wd[c, e], NT) for e in range(local)
        )

    none = tuple(jnp.zeros(gp.shape[1:], F32) for _ in range(local))
    grads = lax.fori_loop(0, chunks, back, none)
    g_gate, g_up = [], []
    for e in range(local):
        g = gp[e]
        s = jax.nn.sigmoid(g)
        g_gate.append((grads[e] * up[e] * s * (1.0 + g * (1.0 - s))).astype(BF))
        g_up.append((grads[e] * (g * s)).astype(BF))

    @pl.loop(0, chunks)
    def _(c):
        parts = []
        for e in range(local):
            r = mm(g_gate[e], wg[c, e], NT) + mm(g_up[e], wu[c, e], NT)
            parts.append(mm(place[e], r.astype(BF)))
        gres[:, cols(c)] = functools.reduce(jnp.add, parts).astype(BF)
    start(3)

    code = codes[...].astype(F32)
    share = code / jnp.sum(code, axis=1, keepdims=True)
    mix = functools.reduce(jnp.add, [m * share[:, k:k + 1] for k, m in enumerate(marks)])
    high = mix.astype(BF)
    low = (mix - high.astype(F32)).astype(BF)

    finish(2)

    @pl.loop(0, chunks)
    def _(c):
        x = ret[:, cols(c)]
        out[:, cols(c)] = (hid[:, cols(c)].astype(F32) + mm(high, x) + mm(low, x)).astype(BF)

    finish(3)

    def scaling(c, acc):
        x = gret[:, cols(c)]
        a = gain[:, cols(c)] * (mm(high, x) + mm(low, x))
        scaled[:, cols(c)] = a
        return acc + jnp.sum(a * hid[:, cols(c)].astype(F32), axis=1, keepdims=True)

    mean = lax.fori_loop(0, chunks, scaling, zero) / features
    cubed = scale * scale * scale * mean

    @pl.loop(0, chunks)
    def _(c):
        gin[:, cols(c)] = (
            og[:, cols(c)].astype(F32) + scale * scaled[:, cols(c)] - hid[:, cols(c)].astype(F32) * cubed
        ).astype(BF)

    for step in range(4):
        @pl.loop(1, n)
        def _(k, step=step):
            row_copy(step, *flows[step], k).wait_send()
    for i in range(3):
        @pl.loop(1, nb)
        def _(k, i=i):
            to_batch(i, k).wait_send()
        for j in range(nb):
            for k in range(1, nh):
                to_head(i, j, k).wait_send()


def body(hidden_in, norm_gain, w_gate, w_up, w_down, expert_ids, gate_codes, out_grad):
    n, nb, nh = (lax.axis_size(a) for a in ("expert", "batch", "head"))
    local, width, hidden = w_gate.shape
    experts = n * local
    tok, features = hidden_in.shape
    chosen = expert_ids.shape[1]
    cap = 3 * tok * chosen // (2 * experts)
    rows = -(-local * cap // 16) * 16
    chunks = nb * nh
    numbers = np.arange(experts)
    base = (numbers // local * rows + numbers % local * cap).astype(np.float32)[None]
    pick = np.zeros((local, n * cap, n * rows), np.float32)
    for e in range(local):
        line = np.arange(n * cap)
        pick[e, line, line // cap * rows + e * cap + line % cap] = 1.0
    place = pick.transpose(0, 2, 1)
    flow = pltpu.VMEM((n * rows, features), BF)
    vmem = pl.BlockSpec(memory_space=pltpu.VMEM)
    hbm = pl.BlockSpec(memory_space=pl.ANY)
    dma = pltpu.SemaphoreType.DMA
    out_type = jax.ShapeDtypeStruct((tok, features), BF)
    return pl.pallas_call(
        functools.partial(kernel, (n, nb, nh, cap, rows, local)),
        out_shape=(out_type, out_type),
        in_specs=[vmem, vmem, hbm, hbm, hbm] + [vmem] * 6,
        out_specs=(vmem, vmem),
        scratch_shapes=[
            pltpu.VMEM((chunks, local, width, hidden), BF),
            pltpu.VMEM((chunks, local, width, hidden), BF),
            pltpu.VMEM((chunks, local, hidden, width), BF),
        ] + [flow] * 8 + [
            pltpu.VMEM((local, n * cap, hidden), F32),
            pltpu.VMEM((local, n * cap, hidden), F32),
            pltpu.VMEM((tok, features), F32),
            pltpu.VMEM((tok, n * rows), BF),
            dma((4, n)), dma((4, n)), dma((4,)),
            dma((3, nb)), dma((3, nb, nh)), dma((3, chunks)), dma((3,)),
        ],
        compiler_params=pltpu.CompilerParams(
            collective_id=0, has_side_effects=True, vmem_limit_bytes=60 * 1024 * 1024
        ),
    )(
        hidden_in, norm_gain[None], w_gate, w_up, w_down, expert_ids, gate_codes, out_grad,
        jnp.asarray(base), jnp.asarray(pick, BF), jnp.asarray(place, BF),
    )


def solution(mesh):
    tokens = P(("batch", "head", "expert"), None)
    in_specs = (
        tokens,
        P(),
        P("expert", ("batch", "head"), None),
        P("expert", ("batch", "head"), None),
        P("expert", None, ("batch", "head")),
        tokens,
        tokens,
        tokens,
    )
    return jax.shard_map(body, mesh=mesh, in_specs=in_specs, out_specs=(tokens, tokens), check_vma=False)
```

time: 234 us -> 153 us (0.65); the launches traced: 229 us -> 152 us
  Pallas kernels: 0 us -> 146 us
  waiting for transfers between devices: 126 us -> 0 us
  local copies, waits for them, and re-layouts: 33.9 us -> 4.89 us
  starting transfers between devices: 25.4 us -> 0 us
  matrix products: 15.9 us -> 0 us
  other arithmetic: 14 us -> 0 us
  between operations: 14 us -> 0.66 us
    pallas_call x0 -> x1, Pallas kernels: none -> 146 us  [body(): pl.pallas_call(functools.partial(kernel, (n, nb, nh, cap, rows, local)),...]
    all_to_all x4 -> x0, waiting for transfers between devices: 124 us -> none  [the longest x1 34 us: body(): lax.all_to_all(send_normed, 'expert', split_axis=1, concat_axis=1, tiled=...]
    all_to_all x4 -> x0, starting transfers between devices: 25.4 us -> none  [the longest x1 6.77 us: body(): lax.all_to_all(result.reshape(slot_shape), 'expert', split_axis=1, concat...]
    dot_general x6 -> x0, matrix products: 15.9 us -> none  [the longest x1 3.7 us: expert_forward(): up_pre = jnp.dot(slot_rows, up_mat, preferred_element_type=jnp.float32)]
    gather x4 -> x0, local copies, waits for them, and re-layouts: 10.3 us -> none  [the longest x1 3.1 us: body(): out_grad[order_rows]]
    reduce_sum x5 -> x0, other arithmetic: 8.27 us -> none  [the longest x1 7.73 us: body(): grad_normed = jnp.sum(picked_grad * weights[:, :, None], axis=1)]
    all_to_all x4 -> x0, local copies, waits for them, and re-layouts: 7.28 us -> none  [the longest x1 2.76 us: body(): lax.all_to_all(send_grad, 'expert', split_axis=1, concat_axis=1, tiled=True)]
    convert_element_type x2 -> x0, local copies, waits for them, and re-layouts: 6.88 us -> none  [the longest x1 3.49 us: body(): picked = returned.reshape(-1, features)[flat_index].astype(jnp.float32).r...]
  transfers between devices with their start and end apart: 7 -> 0, of which waited for: 4 -> 0; matrix products, arithmetic and copies ran while one was open for 16% -> 0% of each run, Pallas kernels for 0% -> 0%
where the time goes in v1:
time: 153 us; the launch traced here: 152 us
  Pallas kernels  146 us (95%)
  local copies, waits for them, and re-layouts  4.89 us (3%)
    pallas_call x1, Pallas kernels, body(): pl.pallas_call(functools.partial(kernel, (n, nb, nh, cap, rows, local)),...  146 us
    unnamed x10, local copies, waits for them, and re-layouts  4.89 us

profile of v1, /device:TPU:30, one launch (start us, length us, event | category | flops | bytes accessed | tf_op | source)
XLA Modules:
  0.0 152.0 jit_solution(8541787302891106317)
XLA Ops:
  0.6 0.0 copy-start.1
  0.6 0.7 copy-done.1
  1.3 0.0 copy-start.2
  1.3 0.7 copy.13.ids
  2.1 0.0 copy-done.2
  2.1 0.7 copy.14.codes
  2.8 146.5 %shard_map.122 = (bf16[128,2048]{1,0:T(8,128)(2,1)}, bf16[128,2048]{1,0:T(8,128)(2,1)}) custom-call(bf16[128,2048]{1,0:T(8,128)(2,1)} %hid.1, f32[1,2048]{1,0:T(1,128)} %bitcast.1, bf16[2,512,384]{2,1,0:T(8,128)(2,1)} %wg_in.1, bf16[2,512,384]{2,1,0:T(8,128)(2,1)} %wu_in.1, bf16[2,384,512]{2,1,0:T(8,128)(2,1)} %wd_in.1, s32[128,2]{1,0:T(8,128)} %copy.13.ids, ...), custom_call_target="tpu_custom_call" | custom-call | tf_op jit(solution)/shard_map/pallas_call | solution.py:265
  149.3 0.0 copy-start
  149.3 1.9 %copy.17 = bf16[128,2048]{1,0:T(8,128)(2,1)} copy(bf16[128,2048]{1,0:T(8,128)(2,1)} %get-tuple-element.4) | data formatting | bytes 1048576
  151.2 0.0 copy-done
  151.2 0.8 copy.18
Async XLA Ops:
  0.6 0.7 copy-start.1
  1.3 0.7 copy-start.2
  149.3 2.0 %copy-start = (bf16[128,2048]{1,0:T(8,128)(2,1)S(1)}, bf16[128,2048]{1,0:T(8,128)(2,1)}, u32[]{:S(2)}) copy-start(bf16[128,2048]{1,0:T(8,128)(2,1)} %get-tuple-element.5) | copy-start | bytes 1572868

commit v2 on v1

--- a/solution.py
+++ b/solution.py
@@ -22,11 +22,12 @@
 
 
 def kernel(
-    sizes, hid, gain, wg_in, wu_in, wd_in, ids, codes, og, base, pick, place, out, gin,
-    wg, wu, wd, send_n, send_g, recv_n, recv_g, res, gres, ret, gret, gp, up, scaled, table,
-    s_sem, r_sem, own_sem, wb_send, wh_send, w_recv, w_own,
+    sizes, hid, gain, wg_in, wu_in, wd_in, meta, og, base, pick, place, out, gin,
+    wg, wu, wd, send_n, recv_n, recv_g, res, gres, gret, send_g, ret, pass_g, pass_r,
+    far_og, far_part, far_sum, far_meta, gp, up, scaled, table,
+    s_sem, r_sem, pass_send, part_recv, og_sem, sum_sem, meta_sem, wb_send, wh_send, w_recv, w_own,
 ):
-    n, nb, nh, cap, rows, local = sizes
+    n, nb, nh, cap, rows, local, chosen = sizes
     me, mb, mh = (lax.axis_index(a) for a in ("expert", "batch", "head"))
     tok, features = hid.shape
     chunks = nb * nh
@@ -70,6 +71,33 @@
     def keep_own(i):
         return pltpu.make_async_copy(tensors[i][0], tensors[i][1].at[mine], w_own.at[i])
 
+    quarter, half = n // 4, n // 2
+    side, lane, q = me // half, lax.rem(me, quarter), me // quarter
+    first = side * half
+    relays = q == 1 + side
+    turn = (1 - side) * (1 - q) + side * (q - 2)
+    beyond = (2 - side) * quarter + lane
+
+    def source(d):
+        return ((2 - side) + d * (1 - 2 * side)) * quarter + lane
+
+    def remote(src, dst, send, recv, other):
+        return pltpu.make_async_remote_copy(
+            src_ref=src, dst_ref=dst, send_sem=send, recv_sem=recv,
+            device_id={"expert": other}, device_id_type=MESH,
+        )
+
+    def meta_out():
+        return remote(meta, far_meta.at[turn], meta_sem.at[0], meta_sem.at[1 + turn], beyond)
+
+    def og_out():
+        return remote(og, far_og.at[turn], og_sem.at[0], og_sem.at[1 + turn], beyond)
+
+    def wait(ref, sem):
+        pltpu.make_async_copy(ref, ref, sem).wait()
+
+    meta_out().start()
+    og_out().start()
     for i in range(3):
         @pl.loop(1, nb)
         def _(k, i=i):
@@ -79,48 +107,84 @@
     def block(ref, d):
         return ref.at[pl.ds(pl.multiple_of(d * rows, 16), rows)]
 
-    def row_copy(step, src, dst, k):
-        other = lax.rem(me + k, n)
-        return pltpu.make_async_remote_copy(
-            src_ref=block(src, other), dst_ref=block(dst, me),
-            send_sem=s_sem.at[step, k], recv_sem=r_sem.at[step, k],
-            device_id={"expert": other}, device_id_type=MESH,
+    def near(k):
+        return first + lax.rem(me - first + k, half)
+
+    def direct(step, k):
+        if step == 0 or step == 3:
+            src, dst = ((send_n, recv_n), None, None, (gres, gret))[step]
+            other = lax.rem(me + k, n)
+            src, dst = block(src, other), block(dst, me)
+        elif step == 1:
+            other = near(k)
+            src, dst = block(send_g, other - first), block(recv_g, me)
+        else:
+            other = near(k)
+            src, dst = block(res, other), block(ret, me - first)
+        return remote(src, dst, s_sem.at[step, other], r_sem.at[step, me], other)
+
+    homes = ((send_n, recv_n), (send_g, recv_g), (res, ret), (gres, gret))
+    spans = (n, half, half, n)
+
+    def start(step):
+        @pl.loop(1, spans[step])
+        def _(k):
+            direct(step, k).start()
+        src, dst = homes[step]
+        at = (me, me - first, me, me)[step], (me, me, me - first, me)[step]
+        pltpu.make_async_copy(block(src, at[0]), block(dst, at[1]), r_sem.at[step, me]).start()
+
+    def finish(step):
+        dst = homes[step][1]
+        @pl.loop(0, half if step == 2 else n)
+        def _(j):
+            wait(block(dst, j), r_sem.at[step, j + first if step == 2 else j])
+
+    def pass_on(d, k):
+        other = near(k)
+        return remote(
+            block(pass_g.at[d], other - first), block(recv_g, source(d)),
+            pass_send.at[0, d, k], r_sem.at[1, source(d)], other,
         )
 
-    flows = ((send_n, recv_n), (send_g, recv_g), (res, ret), (gres, gret))
-
-    def own_copy(step):
-        src, dst = flows[step]
-        return pltpu.make_async_copy(block(src, me), block(dst, me), own_sem.at[step])
-
-    def start(step):
-        @pl.loop(1, n)
-        def _(k):
-            row_copy(step, *flows[step], k).start()
-        own_copy(step).start()
-
-    def finish(step):
-        @pl.loop(1, n)
-        def _(k):
-            dst = block(flows[step][1], lax.rem(me + n - k, n))
-            pltpu.make_async_copy(dst, dst, r_sem.at[step, k]).wait()
-        own_copy(step).wait()
+    def to_relay(k):
+        s = half - first + k
+        qs = s // quarter
+        d = side * (1 - qs) + (1 - side) * (qs - 2)
+        other = (1 + side) * quarter + lax.rem(s, quarter)
+        src, dst = block(res, s), block(pass_r.at[d], me - first)
+        recv = part_recv.at[d, me - first]
+        return other, src, dst, s_sem.at[2, s], recv
+
+    def sum_out(d):
+        return remote(far_sum.at[d], far_part, pass_send.at[1, d, 0], sum_sem.at[0], source(d))
 
     def cols(c):
         return pl.ds(pl.multiple_of(c * width, 128), width)
 
-    experts = base.shape[1]
-    chosen = ids.shape[1]
-    lanes = lax.broadcasted_iota(jnp.int32, (tok, experts), 1)
-    hits = [(ids[:, k:k + 1] == lanes).astype(F32) for k in range(chosen)]
-    total = functools.reduce(jnp.add, hits)
-    earlier = (
-        lax.broadcasted_iota(jnp.int32, (tok, tok), 1) < lax.broadcasted_iota(jnp.int32, (tok, tok), 0)
+    experts = base.shape[0]
+    lower = (
+        lax.broadcasted_iota(jnp.int32, (tok, tok), 0) < lax.broadcasted_iota(jnp.int32, (tok, tok), 1)
     ).astype(F32).astype(BF)
-    where = mm(earlier, total.astype(BF)) + base[...]
-    slots = lax.broadcasted_iota(jnp.int32, (tok, n * rows), 1).astype(F32)
-    marks = [(slots == jnp.sum(where * h, axis=1, keepdims=True)).astype(F32) for h in hits]
-    table[...] = functools.reduce(jnp.add, marks).astype(BF)
+
+    def routing(words, begin, count):
+        labels = lax.broadcasted_iota(jnp.int32, (experts, tok), 0)
+        hits = [(words[k:k + 1] == labels).astype(F32) for k in range(chosen)]
+        where = mm(functools.reduce(jnp.add, hits).astype(BF), lower) + base[...]
+        slots = (lax.broadcasted_iota(jnp.int32, (count, tok), 0) + begin).astype(F32)
+        marks = [(slots == jnp.sum(where * h, axis=0, keepdims=True)).astype(F32) for h in hits]
+        code = [words[chosen + k:chosen + k + 1].astype(F32) for k in range(chosen)]
+        total = functools.reduce(jnp.add, code)
+        mix = functools.reduce(jnp.add, [m * (w / total) for m, w in zip(marks, code)])
+        high = mix.astype(BF)
+        low = (mix - high.astype(F32)).astype(BF)
+        return functools.reduce(jnp.add, marks).astype(BF), high, low
+
+    def combine(high, low, x):
+        return mm(high, x, TN) + mm(low, x, TN)
+
+    table[0], table[1], table[2] = routing(meta[...], 0, n * rows)
+    own = pl.ds(pl.multiple_of(first * rows, 16), half * rows)
 
     def square(c, acc):
         v = hid[:, cols(c)].astype(F32)
@@ -132,27 +196,52 @@
     @pl.loop(0, chunks)
     def _(c):
         v = (hid[:, cols(c)].astype(F32) * scale * gain[:, cols(c)]).astype(BF)
-        send_n[:, cols(c)] = mm(table[...], v, TN).astype(BF)
+        send_n[:, cols(c)] = mm(table[0], v).astype(BF)
     start(0)
 
     @pl.loop(0, chunks)
     def _(c):
-        send_g[:, cols(c)] = mm(table[...], og[:, cols(c)], TN).astype(BF)
+        send_g[:, cols(c)] = mm(table[0, own], og[:, cols(c)]).astype(BF)
     start(1)
 
-    for i in range(3):
+    def forward_on(i):
         for j in range(nb):
             if j > 0:
                 arrived(i, lax.rem(mb + j, nb) * nh + mh)
             for k in range(1, nh):
                 to_head(i, j, k).start()
-    for i in range(3):
+
+    def whole(i):
         keep_own(i).wait()
         for b in range(nb):
             for k in range(1, nh):
                 arrived(i, b * nh + lax.rem(mh + k, nh))
 
+    forward_on(0)
+
+    @pl.when(relays)
+    def _():
+        for d in range(2):
+            wait(far_meta.at[d], meta_sem.at[1 + d])
+            wait(far_og.at[d], og_sem.at[1 + d])
+            spread = routing(far_meta[d], first * rows, half * rows)[0]
+
+            @pl.loop(0, chunks)
+            def _(c, d=d, spread=spread):
+                pass_g[d, :, cols(c)] = mm(spread, far_og[d, :, cols(c)]).astype(BF)
+
+            @pl.loop(1, half)
+            def _(k, d=d):
+                pass_on(d, k).start()
+            pltpu.make_async_copy(
+                block(pass_g.at[d], me - first), block(recv_g, source(d)), r_sem.at[1, source(d)]
+            ).start()
+
+    forward_on(1)
+    forward_on(2)
     finish(0)
+    whole(0)
+    whole(1)
     gp[...] = jnp.zeros_like(gp)
     up[...] = jnp.zeros_like(up)
 
@@ -164,12 +253,25 @@
             gp[e] += mm(xe, wg[c, e])
             up[e] += mm(xe, wu[c, e])
 
+    whole(2)
     inner = [(jax.nn.silu(gp[e]) * up[e]).astype(BF) for e in range(local)]
 
     @pl.loop(0, chunks)
     def _(c):
         parts = [mm(place[e], mm(inner[e], wd[c, e]).astype(BF)) for e in range(local)]
         res[:, cols(c)] = functools.reduce(jnp.add, parts).astype(BF)
+
+    @pl.loop(0, half)
+    def _(k):
+        other, src, dst, send, recv = to_relay(k)
+
+        @pl.when(other != me)
+        def _():
+            remote(src, dst, send, recv, other).start()
+
+        @pl.when(other == me)
+        def _():
+            pltpu.make_async_copy(src, dst, recv).start()
     start(2)
 
     finish(1)
@@ -198,24 +300,32 @@
         gres[:, cols(c)] = functools.reduce(jnp.add, parts).astype(BF)
     start(3)
 
-    code = codes[...].astype(F32)
-    share = code / jnp.sum(code, axis=1, keepdims=True)
-    mix = functools.reduce(jnp.add, [m * share[:, k:k + 1] for k, m in enumerate(marks)])
-    high = mix.astype(BF)
-    low = (mix - high.astype(F32)).astype(BF)
+    @pl.when(relays)
+    def _():
+        for d in range(2):
+            @pl.loop(0, half)
+            def _(j, d=d):
+                wait(block(pass_r.at[d], j), part_recv.at[d, j])
+            _, high, low = routing(far_meta[d], first * rows, half * rows)
+
+            @pl.loop(0, chunks)
+            def _(c, d=d, high=high, low=low):
+                far_sum[d, :, cols(c)] = combine(high, low, pass_r[d, :, cols(c)]).astype(BF)
+            sum_out(d).start()
 
     finish(2)
-
-    @pl.loop(0, chunks)
-    def _(c):
-        x = ret[:, cols(c)]
-        out[:, cols(c)] = (hid[:, cols(c)].astype(F32) + mm(high, x) + mm(low, x)).astype(BF)
+    wait(far_part, sum_sem.at[0])
+
+    @pl.loop(0, chunks)
+    def _(c):
+        mixture = combine(table[1, own], table[2, own], ret[:, cols(c)]) + far_part[:, cols(c)].astype(F32)
+        out[:, cols(c)] = (hid[:, cols(c)].astype(F32) + mixture).astype(BF)
 
     finish(3)
 
     def scaling(c, acc):
         x = gret[:, cols(c)]
-        a = gain[:, cols(c)] * (mm(high, x) + mm(low, x))
+        a = gain[:, cols(c)] * combine(table[1], table[2], x)
         scaled[:, cols(c)] = a
         return acc + jnp.sum(a * hid[:, cols(c)].astype(F32), axis=1, keepdims=True)
 
@@ -229,9 +339,28 @@
         ).astype(BF)
 
     for step in range(4):
-        @pl.loop(1, n)
+        @pl.loop(1, spans[step])
         def _(k, step=step):
-            row_copy(step, *flows[step], k).wait_send()
+            direct(step, k).wait_send()
+
+    @pl.loop(0, half)
+    def _(k):
+        other, src, dst, send, recv = to_relay(k)
+
+        @pl.when(other != me)
+        def _():
+            remote(src, dst, send, recv, other).wait_send()
+    meta_out().wait_send()
+    og_out().wait_send()
+
+    @pl.when(relays)
+    def _():
+        for d in range(2):
+            @pl.loop(1, half)
+            def _(k, d=d):
+                pass_on(d, k).wait_send()
+            sum_out(d).wait_send()
+
     for i in range(3):
         @pl.loop(1, nb)
         def _(k, i=i):
@@ -250,8 +379,10 @@
     cap = 3 * tok * chosen // (2 * experts)
     rows = -(-local * cap // 16) * 16
     chunks = nb * nh
+    meta = jnp.concatenate([expert_ids, gate_codes], axis=1).T
+    meta = jnp.pad(meta, ((0, -2 * chosen % 8), (0, 0)))
     numbers = np.arange(experts)
-    base = (numbers // local * rows + numbers % local * cap).astype(np.float32)[None]
+    base = (numbers // local * rows + numbers % local * cap).astype(np.float32)[:, None]
     pick = np.zeros((local, n * cap, n * rows), np.float32)
     for e in range(local):
         line = np.arange(n * cap)
@@ -263,27 +394,36 @@
     dma = pltpu.SemaphoreType.DMA
     out_type = jax.ShapeDtypeStruct((tok, features), BF)
     return pl.pallas_call(
-        functools.partial(kernel, (n, nb, nh, cap, rows, local)),
+        functools.partial(kernel, (n, nb, nh, cap, rows, local, chosen)),
         out_shape=(out_type, out_type),
-        in_specs=[vmem, vmem, hbm, hbm, hbm] + [vmem] * 6,
+        in_specs=[vmem, vmem, hbm, hbm, hbm] + [vmem] * 5,
         out_specs=(vmem, vmem),
         scratch_shapes=[
             pltpu.VMEM((chunks, local, width, hidden), BF),
             pltpu.VMEM((chunks, local, width, hidden), BF),
             pltpu.VMEM((chunks, local, hidden, width), BF),
-        ] + [flow] * 8 + [
+        ] + [flow] * 6 + [
+            pltpu.VMEM((n // 2 * rows, features), BF),
+            pltpu.VMEM((n // 2 * rows, features), BF),
+            pltpu.VMEM((2, n // 2 * rows, features), BF),
+            pltpu.VMEM((2, n // 2 * rows, features), BF),
+            pltpu.VMEM((2, tok, features), BF),
+            pltpu.VMEM((tok, features), BF),
+            pltpu.VMEM((2, tok, features), BF),
+            pltpu.VMEM((2,) + meta.shape, jnp.int32),
             pltpu.VMEM((local, n * cap, hidden), F32),
             pltpu.VMEM((local, n * cap, hidden), F32),
             pltpu.VMEM((tok, features), F32),
-            pltpu.VMEM((tok, n * rows), BF),
-            dma((4, n)), dma((4, n)), dma((4,)),
+            pltpu.VMEM((3, n * rows, tok), BF),
+            dma((4, n)), dma((4, n)), dma((2, 2, n // 2)), dma((2, n // 2)),
+            dma((3,)), dma((1,)), dma((3,)),
             dma((3, nb)), dma((3, nb, nh)), dma((3, chunks)), dma((3,)),
         ],
         compiler_params=pltpu.CompilerParams(
             collective_id=0, has_side_effects=True, vmem_limit_bytes=60 * 1024 * 1024
         ),
     )(
-        hidden_in, norm_gain[None], w_gate, w_up, w_down, expert_ids, gate_codes, out_grad,
+        hidden_in, norm_gain[None], w_gate, w_up, w_down, meta, out_grad,
         jnp.asarray(base), jnp.asarray(pick, BF), jnp.asarray(place, BF),
     )
 

time: 153 us -> 149 us (0.974)
  Pallas kernels: 146 us -> 143 us
    pallas_call x1, Pallas kernels: 146 us -> 143 us  [body(): pl.pallas_call(functools.partial(kernel, (n, nb, nh, cap, rows, local, ch...]
    unnamed x10 -> x6, local copies, waits for them, and re-layouts: 4.89 us -> 3.41 us
where the time goes in v2:
time: 149 us; the launch traced here: 148 us
  Pallas kernels  143 us (96%)
  local copies, waits for them, and re-layouts  4.01 us (3%)
    pallas_call x1, Pallas kernels, body(): pl.pallas_call(functools.partial(kernel, (n, nb, nh, cap, rows, local, ch...  143 us
    unnamed x6, local copies, waits for them, and re-layouts  3.41 us

profile of v2, /device:TPU:30, one launch (start us, length us, event | category | flops | bytes accessed | tf_op | source)
XLA Modules:
  0.0 148.4 jit_solution(5068406009479235241)
XLA Ops:
  0.6 0.0 copy-start.1
  0.6 0.7 copy-done.1
  1.3 0.7 add_bitcast_fusion
  2.0 0.6 pad.4.meta
  2.6 143.1 %shard_map.122 = (bf16[128,2048]{1,0:T(8,128)(2,1)}, bf16[128,2048]{1,0:T(8,128)(2,1)}) custom-call(bf16[128,2048]{1,0:T(8,128)(2,1)} %hid.1, f32[1,2048]{1,0:T(1,128)} %bitcast.3, bf16[2,512,384]{2,1,0:T(8,128)(2,1)} %wg_in.1, bf16[2,512,384]{2,1,0:T(8,128)(2,1)} %wu_in.1, bf16[2,384,512]{2,1,0:T(8,128)(2,1)} %wd_in.1, s32[8,128]{1,0:T(8,128)} %pad.4.meta, ...), custom_call_target="tpu_custom_call" | custom-call | tf_op jit(solution)/shard_map/pallas_call | solution.py:396
  145.7 0.0 copy-start
  145.7 1.9 %copy.15 = bf16[128,2048]{1,0:T(8,128)(2,1)} copy(bf16[128,2048]{1,0:T(8,128)(2,1)} %get-tuple-element.4) | data formatting | bytes 1048576
  147.6 0.0 copy-done
  147.6 0.8 copy.16
Async XLA Ops:
  0.6 0.7 copy-start.1
  145.7 2.0 %copy-start = (bf16[128,2048]{1,0:T(8,128)(2,1)S(1)}, bf16[128,2048]{1,0:T(8,128)(2,1)}, u32[]{:S(2)}) copy-start(bf16[128,2048]{1,0:T(8,128)(2,1)} %get-tuple-element.5) | copy-start | bytes 1572868

commit v3 on v2

--- a/solution.py
+++ b/solution.py
@@ -23,9 +23,9 @@
 
 def kernel(
     sizes, hid, gain, wg_in, wu_in, wd_in, meta, og, base, pick, place, out, gin,
-    wg, wu, wd, send_n, recv_n, recv_g, res, gres, gret, send_g, ret, pass_g, pass_r,
-    far_og, far_part, far_sum, far_meta, gp, up, scaled, table,
-    s_sem, r_sem, pass_send, part_recv, og_sem, sum_sem, meta_sem, wb_send, wh_send, w_recv, w_own,
+    wg, wu, wd, send_n, recv_n, recv_g, res, gres, ret, send_g, gret, pass_g, pass_r,
+    far_og, far_part, far_sum, far_meta, far_table, gp, up, scaled, table,
+    s_sem, r_sem, near_sem, pass_send, part_send, part_recv, og_sem, sum_send, sum_recv, meta_sem, wb_send, wh_send, w_recv, w_own,
 ):
     n, nb, nh, cap, rows, local, chosen = sizes
     me, mb, mh = (lax.axis_index(a) for a in ("expert", "batch", "head"))
@@ -78,6 +78,9 @@
     turn = (1 - side) * (1 - q) + side * (q - 2)
     beyond = (2 - side) * quarter + lane
 
+    def cols(c):
+        return pl.ds(pl.multiple_of(c * width, 128), width)
+
     def source(d):
         return ((2 - side) + d * (1 - 2 * side)) * quarter + lane
 
@@ -90,14 +93,15 @@
     def meta_out():
         return remote(meta, far_meta.at[turn], meta_sem.at[0], meta_sem.at[1 + turn], beyond)
 
-    def og_out():
-        return remote(og, far_og.at[turn], og_sem.at[0], og_sem.at[1 + turn], beyond)
+    def og_out(c):
+        return remote(
+            og.at[:, cols(c)], far_og.at[turn, :, cols(c)], og_sem.at[0, c], og_sem.at[1 + turn, c], beyond
+        )
 
     def wait(ref, sem):
         pltpu.make_async_copy(ref, ref, sem).wait()
 
     meta_out().start()
-    og_out().start()
     for i in range(3):
         @pl.loop(1, nb)
         def _(k, i=i):
@@ -111,56 +115,62 @@
         return first + lax.rem(me - first + k, half)
 
     def direct(step, k):
-        if step == 0 or step == 3:
-            src, dst = ((send_n, recv_n), None, None, (gres, gret))[step]
-            other = lax.rem(me + k, n)
-            src, dst = block(src, other), block(dst, me)
-        elif step == 1:
-            other = near(k)
+        other = near(k)
+        if step == 1:
             src, dst = block(send_g, other - first), block(recv_g, me)
         else:
-            other = near(k)
-            src, dst = block(res, other), block(ret, me - first)
+            other = lax.rem(me + 1 + lax.rem(k + half - 2, n - 1), n)
+            src, dst = ((send_n, recv_n), None, (res, ret))[step]
+            src, dst = block(src, other), block(dst, me)
         return remote(src, dst, s_sem.at[step, other], r_sem.at[step, me], other)
 
-    homes = ((send_n, recv_n), (send_g, recv_g), (res, ret), (gres, gret))
-    spans = (n, half, half, n)
+    homes = ((send_n, recv_n), (send_g, recv_g), (res, ret))
+    spans = (n, half, n)
 
     def start(step):
         @pl.loop(1, spans[step])
         def _(k):
             direct(step, k).start()
         src, dst = homes[step]
-        at = (me, me - first, me, me)[step], (me, me, me - first, me)[step]
-        pltpu.make_async_copy(block(src, at[0]), block(dst, at[1]), r_sem.at[step, me]).start()
+        at = me - first if step == 1 else me
+        pltpu.make_async_copy(block(src, at), block(dst, me), r_sem.at[step, me]).start()
 
     def finish(step):
         dst = homes[step][1]
-        @pl.loop(0, half if step == 2 else n)
+
+        @pl.loop(0, n)
         def _(j):
-            wait(block(dst, j), r_sem.at[step, j + first if step == 2 else j])
-
-    def pass_on(d, k):
+            wait(block(dst, j), r_sem.at[step, j])
+
+    def piece(ref, j, c):
+        return ref.at[pl.ds(pl.multiple_of(j * rows, 16), rows), cols(c)]
+
+    def near_out(k, c):
         other = near(k)
         return remote(
-            block(pass_g.at[d], other - first), block(recv_g, source(d)),
-            pass_send.at[0, d, k], r_sem.at[1, source(d)], other,
-        )
-
-    def to_relay(k):
+            piece(gres, other, c), piece(gret, me - first, c),
+            near_sem.at[0, k, c], near_sem.at[1, me - first, c], other,
+        )
+
+    def pass_on(d, k, c):
+        other = near(k)
+        return remote(
+            piece(pass_g.at[d], other - first, c), piece(recv_g, source(d), c),
+            pass_send.at[d, k, c], r_sem.at[1, source(d)], other,
+        )
+
+    def to_relay(k, c):
         s = half - first + k
         qs = s // quarter
         d = side * (1 - qs) + (1 - side) * (qs - 2)
         other = (1 + side) * quarter + lax.rem(s, quarter)
-        src, dst = block(res, s), block(pass_r.at[d], me - first)
-        recv = part_recv.at[d, me - first]
-        return other, src, dst, s_sem.at[2, s], recv
-
-    def sum_out(d):
-        return remote(far_sum.at[d], far_part, pass_send.at[1, d, 0], sum_sem.at[0], source(d))
-
-    def cols(c):
-        return pl.ds(pl.multiple_of(c * width, 128), width)
+        src, dst = piece(gres, s, c), piece(pass_r.at[d], me - first, c)
+        return other, src, dst, part_send.at[k, c], part_recv.at[d, me - first, c]
+
+    def sum_out(d, c):
+        return remote(
+            far_sum.at[d, :, cols(c)], far_part.at[:, cols(c)], sum_send.at[d, c], sum_recv.at[c], source(d)
+        )
 
     experts = base.shape[0]
     lower = (
@@ -201,6 +211,10 @@
 
     @pl.loop(0, chunks)
     def _(c):
+        og_out(c).start()
+
+    @pl.loop(0, chunks)
+    def _(c):
         send_g[:, cols(c)] = mm(table[0, own], og[:, cols(c)]).astype(BF)
     start(1)
 
@@ -218,27 +232,7 @@
                 arrived(i, b * nh + lax.rem(mh + k, nh))
 
     forward_on(0)
-
-    @pl.when(relays)
-    def _():
-        for d in range(2):
-            wait(far_meta.at[d], meta_sem.at[1 + d])
-            wait(far_og.at[d], og_sem.at[1 + d])
-            spread = routing(far_meta[d], first * rows, half * rows)[0]
-
-            @pl.loop(0, chunks)
-            def _(c, d=d, spread=spread):
-                pass_g[d, :, cols(c)] = mm(spread, far_og[d, :, cols(c)]).astype(BF)
-
-            @pl.loop(1, half)
-            def _(k, d=d):
-                pass_on(d, k).start()
-            pltpu.make_async_copy(
-                block(pass_g.at[d], me - first), block(recv_g, source(d)), r_sem.at[1, source(d)]
-            ).start()
-
     forward_on(1)
-    forward_on(2)
     finish(0)
     whole(0)
     whole(1)
@@ -253,6 +247,31 @@
             gp[e] += mm(xe, wg[c, e])
             up[e] += mm(xe, wu[c, e])
 
+    @pl.when(relays)
+    def _():
+        for d in range(2):
+            wait(far_meta.at[d], meta_sem.at[1 + d])
+            far_table[d, 0], far_table[d, 1], far_table[d, 2] = routing(far_meta[d], first * rows, half * rows)
+
+    def relay_grads(begin, end):
+        @pl.when(relays)
+        def _():
+            @pl.loop(begin, end)
+            def _(c):
+                for d in range(2):
+                    wait(far_og.at[d, :, cols(c)], og_sem.at[1 + d, c])
+                    pass_g[d, :, cols(c)] = mm(far_table[d, 0], far_og[d, :, cols(c)]).astype(BF)
+
+                    @pl.loop(1, half)
+                    def _(k, d=d):
+                        pass_on(d, k, c).start()
+                    pltpu.make_async_copy(
+                        piece(pass_g.at[d], me - first, c), piece(recv_g, source(d), c), r_sem.at[1, source(d)]
+                    ).start()
+
+    relay_grads(0, chunks // 2)
+    forward_on(2)
+    relay_grads(chunks // 2, chunks)
     whole(2)
     inner = [(jax.nn.silu(gp[e]) * up[e]).astype(BF) for e in range(local)]
 
@@ -260,18 +279,6 @@
     def _(c):
         parts = [mm(place[e], mm(inner[e], wd[c, e]).astype(BF)) for e in range(local)]
         res[:, cols(c)] = functools.reduce(jnp.add, parts).astype(BF)
-
-    @pl.loop(0, half)
-    def _(k):
-        other, src, dst, send, recv = to_relay(k)
-
-        @pl.when(other != me)
-        def _():
-            remote(src, dst, send, recv, other).start()
-
-        @pl.when(other == me)
-        def _():
-            pltpu.make_async_copy(src, dst, recv).start()
     start(2)
 
     finish(1)
@@ -298,34 +305,56 @@
             r = mm(g_gate[e], wg[c, e], NT) + mm(g_up[e], wu[c, e], NT)
             parts.append(mm(place[e], r.astype(BF)))
         gres[:, cols(c)] = functools.reduce(jnp.add, parts).astype(BF)
-    start(3)
-
-    @pl.when(relays)
-    def _():
-        for d in range(2):
-            @pl.loop(0, half)
-            def _(j, d=d):
-                wait(block(pass_r.at[d], j), part_recv.at[d, j])
-            _, high, low = routing(far_meta[d], first * rows, half * rows)
-
-            @pl.loop(0, chunks)
-            def _(c, d=d, high=high, low=low):
-                far_sum[d, :, cols(c)] = combine(high, low, pass_r[d, :, cols(c)]).astype(BF)
-            sum_out(d).start()
-
+
+        @pl.loop(0, half)
+        def _(k):
+            other, src, dst, send, recv = to_relay(k, c)
+
+            @pl.when(other != me)
+            def _():
+                remote(src, dst, send, recv, other).start()
+
+            @pl.when(other == me)
+            def _():
+                pltpu.make_async_copy(src, dst, recv).start()
+
+        @pl.loop(1, half)
+        def _(k):
+            near_out(k, c).start()
+        pltpu.make_async_copy(
+            piece(gres, me, c), piece(gret, me - first, c), near_sem.at[1, me - first, c]
+        ).start()
+
+    def relay_sums(begin, end):
+        @pl.when(relays)
+        def _():
+            @pl.loop(begin, end)
+            def _(c):
+                for d in range(2):
+                    @pl.loop(0, half)
+                    def _(j, d=d):
+                        wait(piece(pass_r.at[d], j, c), part_recv.at[d, j, c])
+                    x = pass_r[d, :, cols(c)]
+                    far_sum[d, :, cols(c)] = combine(far_table[d, 1], far_table[d, 2], x).astype(BF)
+                    sum_out(d, c).start()
+
+    relay_sums(0, chunks // 2)
     finish(2)
-    wait(far_part, sum_sem.at[0])
-
-    @pl.loop(0, chunks)
-    def _(c):
-        mixture = combine(table[1, own], table[2, own], ret[:, cols(c)]) + far_part[:, cols(c)].astype(F32)
+
+    @pl.loop(0, chunks)
+    def _(c):
+        mixture = combine(table[1], table[2], ret[:, cols(c)])
         out[:, cols(c)] = (hid[:, cols(c)].astype(F32) + mixture).astype(BF)
 
-    finish(3)
+    relay_sums(chunks // 2, chunks)
 
     def scaling(c, acc):
-        x = gret[:, cols(c)]
-        a = gain[:, cols(c)] * combine(table[1], table[2], x)
+        @pl.loop(0, half)
+        def _(j):
+            wait(piece(gret, j, c), near_sem.at[1, j, c])
+        wait(far_part.at[:, cols(c)], sum_recv.at[c])
+        total = combine(table[1, own], table[2, own], gret[:, cols(c)]) + far_part[:, cols(c)].astype(F32)
+        a = gain[:, cols(c)] * total
         scaled[:, cols(c)] = a
         return acc + jnp.sum(a * hid[:, cols(c)].astype(F32), axis=1, keepdims=True)
 
@@ -338,28 +367,39 @@
             og[:, cols(c)].astype(F32) + scale * scaled[:, cols(c)] - hid[:, cols(c)].astype(F32) * cubed
         ).astype(BF)
 
-    for step in range(4):
+    for step in range(3):
         @pl.loop(1, spans[step])
         def _(k, step=step):
             direct(step, k).wait_send()
 
-    @pl.loop(0, half)
-    def _(k):
-        other, src, dst, send, recv = to_relay(k)
-
-        @pl.when(other != me)
-        def _():
-            remote(src, dst, send, recv, other).wait_send()
+    @pl.loop(0, chunks)
+    def _(c):
+        @pl.loop(0, half)
+        def _(k):
+            other, src, dst, send, recv = to_relay(k, c)
+
+            @pl.when(other != me)
+            def _():
+                remote(src, dst, send, recv, other).wait_send()
+
+        @pl.loop(1, half)
+        def _(k):
+            near_out(k, c).wait_send()
     meta_out().wait_send()
-    og_out().wait_send()
+
+    @pl.loop(0, chunks)
+    def _(c):
+        og_out(c).wait_send()
 
     @pl.when(relays)
     def _():
-        for d in range(2):
-            @pl.loop(1, half)
-            def _(k, d=d):
-                pass_on(d, k).wait_send()
-            sum_out(d).wait_send()
+        @pl.loop(0, chunks)
+        def _(c):
+            for d in range(2):
+                @pl.loop(1, half)
+                def _(k, d=d):
+                    pass_on(d, k, c).wait_send()
+                sum_out(d, c).wait_send()
 
     for i in range(3):
         @pl.loop(1, nb)
@@ -411,12 +451,14 @@
             pltpu.VMEM((tok, features), BF),
             pltpu.VMEM((2, tok, features), BF),
             pltpu.VMEM((2,) + meta.shape, jnp.int32),
+            pltpu.VMEM((2, 3, n // 2 * rows, tok), BF),
             pltpu.VMEM((local, n * cap, hidden), F32),
             pltpu.VMEM((local, n * cap, hidden), F32),
             pltpu.VMEM((tok, features), F32),
             pltpu.VMEM((3, n * rows, tok), BF),
-            dma((4, n)), dma((4, n)), dma((2, 2, n // 2)), dma((2, n // 2)),
-            dma((3,)), dma((1,)), dma((3,)),
+            dma((3, n)), dma((3, n)), dma((2, n // 2, chunks)), dma((2, n // 2, chunks)),
+            dma((n // 2, chunks)), dma((2, n // 2, chunks)), dma((3, chunks)), dma((2, chunks)), dma((chunks,)),
+            dma((3,)),
             dma((3, nb)), dma((3, nb, nh)), dma((3, chunks)), dma((3,)),
         ],
         compiler_params=pltpu.CompilerParams(

time: 149 us -> 138 us (0.926)
  Pallas kernels: 143 us -> 131 us
    pallas_call x1, Pallas kernels: 143 us -> 131 us  [body(): pl.pallas_call(functools.partial(kernel, (n, nb, nh, cap, rows, local, ch...]
where the time goes in v3:
time: 138 us; the launch traced here: 136 us
  Pallas kernels  131 us (95%)
  local copies, waits for them, and re-layouts  4.01 us (3%)
    pallas_call x1, Pallas kernels, body(): pl.pallas_call(functools.partial(kernel, (n, nb, nh, cap, rows, local, ch...  131 us
    unnamed x6, local copies, waits for them, and re-layouts  3.41 us

profile of v3, /device:TPU:30, one launch (start us, length us, event | category | flops | bytes accessed | tf_op | source)
XLA Modules:
  0.0 136.3 jit_solution(6379734740666424163)
XLA Ops:
  0.6 0.0 copy-start.1
  0.6 0.7 copy-done.1
  1.3 0.7 add_bitcast_fusion
  2.0 0.6 pad.4.meta
  2.6 131.0 %shard_map.122 = (bf16[128,2048]{1,0:T(8,128)(2,1)}, bf16[128,2048]{1,0:T(8,128)(2,1)}) custom-call(bf16[128,2048]{1,0:T(8,128)(2,1)} %hid.1, f32[1,2048]{1,0:T(1,128)} %bitcast.3, bf16[2,512,384]{2,1,0:T(8,128)(2,1)} %wg_in.1, bf16[2,512,384]{2,1,0:T(8,128)(2,1)} %wu_in.1, bf16[2,384,512]{2,1,0:T(8,128)(2,1)} %wd_in.1, s32[8,128]{1,0:T(8,128)} %pad.4.meta, ...), custom_call_target="tpu_custom_call" | custom-call | tf_op jit(solution)/shard_map/pallas_call | solution.py:436
  133.6 0.0 copy-start
  133.6 1.9 %copy.15 = bf16[128,2048]{1,0:T(8,128)(2,1)} copy(bf16[128,2048]{1,0:T(8,128)(2,1)} %get-tuple-element.4) | data formatting | bytes 1048576
  135.5 0.0 copy-done
  135.5 0.8 copy.16
Async XLA Ops:
  0.6 0.7 copy-start.1
  133.6 2.0 %copy-start = (bf16[128,2048]{1,0:T(8,128)(2,1)S(1)}, bf16[128,2048]{1,0:T(8,128)(2,1)}, u32[]{:S(2)}) copy-start(bf16[128,2048]{1,0:T(8,128)(2,1)} %get-tuple-element.5) | copy-start | bytes 1572868

commit v4 on v3

--- a/solution.py
+++ b/solution.py
@@ -101,7 +101,12 @@
     def wait(ref, sem):
         pltpu.make_async_copy(ref, ref, sem).wait()
 
+    early = chunks // 4
     meta_out().start()
+
+    @pl.loop(0, early)
+    def _(c):
+        og_out(c).start()
     for i in range(3):
         @pl.loop(1, nb)
         def _(k, i=i):
@@ -209,7 +214,7 @@
         send_n[:, cols(c)] = mm(table[0], v).astype(BF)
     start(0)
 
-    @pl.loop(0, chunks)
+    @pl.loop(early, chunks)
     def _(c):
         og_out(c).start()
 

time: 138 us -> 137 us (level)
  no operation moved by 1% of the time
where the time goes in v4:
time: 137 us; the launch traced here: 136 us
  Pallas kernels  130 us (95%)
  local copies, waits for them, and re-layouts  4.01 us (3%)
    pallas_call x1, Pallas kernels, body(): pl.pallas_call(functools.partial(kernel, (n, nb, nh, cap, rows, local, ch...  130 us
    unnamed x6, local copies, waits for them, and re-layouts  3.41 us

profile of v4, /device:TPU:30, one launch (start us, length us, event | category | flops | bytes accessed | tf_op | source)
XLA Modules:
  0.0 135.7 jit_solution(13409335398135471101)
XLA Ops:
  0.6 0.0 copy-start.1
  0.6 0.7 copy-done.1
  1.3 0.7 add_bitcast_fusion
  2.0 0.6 pad.4.meta
  2.6 130.4 %shard_map.122 = (bf16[128,2048]{1,0:T(8,128)(2,1)}, bf16[128,2048]{1,0:T(8,128)(2,1)}) custom-call(bf16[128,2048]{1,0:T(8,128)(2,1)} %hid.1, f32[1,2048]{1,0:T(1,128)} %bitcast.3, bf16[2,512,384]{2,1,0:T(8,128)(2,1)} %wg_in.1, bf16[2,512,384]{2,1,0:T(8,128)(2,1)} %wu_in.1, bf16[2,384,512]{2,1,0:T(8,128)(2,1)} %wd_in.1, s32[8,128]{1,0:T(8,128)} %pad.4.meta, ...), custom_call_target="tpu_custom_call" | custom-call | tf_op jit(solution)/shard_map/pallas_call | solution.py:441
  133.0 0.0 copy-start
  133.0 1.9 %copy.15 = bf16[128,2048]{1,0:T(8,128)(2,1)} copy(bf16[128,2048]{1,0:T(8,128)(2,1)} %get-tuple-element.4) | data formatting | bytes 1048576
  134.9 0.0 copy-done
  134.9 0.8 copy.16
Async XLA Ops:
  0.6 0.7 copy-start.1
  133.0 2.0 %copy-start = (bf16[128,2048]{1,0:T(8,128)(2,1)S(1)}, bf16[128,2048]{1,0:T(8,128)(2,1)}, u32[]{:S(2)}) copy-start(bf16[128,2048]{1,0:T(8,128)(2,1)} %get-tuple-element.5) | copy-start | bytes 1572868

commit v5 on v4

--- a/solution.py
+++ b/solution.py
@@ -119,7 +119,7 @@
     def near(k):
         return first + lax.rem(me - first + k, half)
 
-    def direct(step, k):
+    def direct(step, k, c=None):
         other = near(k)
         if step == 1:
             src, dst = block(send_g, other - first), block(recv_g, me)
@@ -127,15 +127,19 @@
             other = lax.rem(me + 1 + lax.rem(k + half - 2, n - 1), n)
             src, dst = ((send_n, recv_n), None, (res, ret))[step]
             src, dst = block(src, other), block(dst, me)
+        if c is not None:
+            src, dst = src.at[:, cols(c)], dst.at[:, cols(c)]
         return remote(src, dst, s_sem.at[step, other], r_sem.at[step, me], other)
 
     homes = ((send_n, recv_n), (send_g, recv_g), (res, ret))
     spans = (n, half, n)
 
-    def start(step):
+    def stream(step, c):
         @pl.loop(1, spans[step])
         def _(k):
-            direct(step, k).start()
+            direct(step, k, c).start()
+
+    def keep(step):
         src, dst = homes[step]
         at = me - first if step == 1 else me
         pltpu.make_async_copy(block(src, at), block(dst, me), r_sem.at[step, me]).start()
@@ -212,7 +216,8 @@
     def _(c):
         v = (hid[:, cols(c)].astype(F32) * scale * gain[:, cols(c)]).astype(BF)
         send_n[:, cols(c)] = mm(table[0], v).astype(BF)
-    start(0)
+        stream(0, c)
+    keep(0)
 
     @pl.loop(early, chunks)
     def _(c):
@@ -221,7 +226,8 @@
     @pl.loop(0, chunks)
     def _(c):
         send_g[:, cols(c)] = mm(table[0, own], og[:, cols(c)]).astype(BF)
-    start(1)
+        stream(1, c)
+    keep(1)
 
     def forward_on(i):
         for j in range(nb):
@@ -284,7 +290,8 @@
     def _(c):
         parts = [mm(place[e], mm(inner[e], wd[c, e]).astype(BF)) for e in range(local)]
         res[:, cols(c)] = functools.reduce(jnp.add, parts).astype(BF)
-    start(2)
+        stream(2, c)
+    keep(2)
 
     finish(1)
 

time: 137 us -> 134 us (0.978)
  Pallas kernels: 130 us -> 127 us
    pallas_call x1, Pallas kernels: 130 us -> 127 us  [body(): pl.pallas_call(functools.partial(kernel, (n, nb, nh, cap, rows, local, ch...]
where the time goes in v5:
time: 134 us; the launch traced here: 133 us
  Pallas kernels  127 us (95%)
  local copies, waits for them, and re-layouts  4.01 us (3%)
    pallas_call x1, Pallas kernels, body(): pl.pallas_call(functools.partial(kernel, (n, nb, nh, cap, rows, local, ch...  127 us
    unnamed x6, local copies, waits for them, and re-layouts  3.41 us

profile of v5, /device:TPU:30, one launch (start us, length us, event | category | flops | bytes accessed | tf_op | source)
XLA Modules:
  0.0 132.8 jit_solution(14127575054134377357)
XLA Ops:
  0.6 0.0 copy-start.1
  0.6 0.7 copy-done.1
  1.3 0.7 add_bitcast_fusion
  2.0 0.6 pad.4.meta
  2.6 127.4 %shard_map.122 = (bf16[128,2048]{1,0:T(8,128)(2,1)}, bf16[128,2048]{1,0:T(8,128)(2,1)}) custom-call(bf16[128,2048]{1,0:T(8,128)(2,1)} %hid.1, f32[1,2048]{1,0:T(1,128)} %bitcast.3, bf16[2,512,384]{2,1,0:T(8,128)(2,1)} %wg_in.1, bf16[2,512,384]{2,1,0:T(8,128)(2,1)} %wu_in.1, bf16[2,384,512]{2,1,0:T(8,128)(2,1)} %wd_in.1, s32[8,128]{1,0:T(8,128)} %pad.4.meta, ...), custom_call_target="tpu_custom_call" | custom-call | tf_op jit(solution)/shard_map/pallas_call | solution.py:448
  130.0 0.0 copy-start
  130.0 1.9 %copy.15 = bf16[128,2048]{1,0:T(8,128)(2,1)} copy(bf16[128,2048]{1,0:T(8,128)(2,1)} %get-tuple-element.4) | data formatting | bytes 1048576
  132.0 0.0 copy-done
  132.0 0.8 copy.16
Async XLA Ops:
  0.6 0.7 copy-start.1
  130.0 2.0 %copy-start = (bf16[128,2048]{1,0:T(8,128)(2,1)S(1)}, bf16[128,2048]{1,0:T(8,128)(2,1)}, u32[]{:S(2)}) copy-start(bf16[128,2048]{1,0:T(8,128)(2,1)} %get-tuple-element.5) | copy-start | bytes 1572868

commit v6 on v5

--- a/solution.py
+++ b/solution.py
@@ -330,6 +330,8 @@
             def _():
                 pltpu.make_async_copy(src, dst, recv).start()
 
+    @pl.loop(0, chunks)
+    def _(c):
         @pl.loop(1, half)
         def _(k):
             near_out(k, c).start()

time: 134 us -> 134 us (level)
  the two profiles are of different devices: /device:TPU:30 before, /device:TPU:0 now
where the time goes in v6:
time: 134 us
  Pallas kernels  129 us (96%)
  local copies, waits for them, and re-layouts  4.01 us (3%)
    pallas_call x1, Pallas kernels, body(): pl.pallas_call(functools.partial(kernel, (n, nb, nh, cap, rows, local, ch...  129 us
    unnamed x6, local copies, waits for them, and re-layouts  3.41 us

profile of v6, /device:TPU:0, one launch (start us, length us, event | category | flops | bytes accessed | tf_op | source)
XLA Modules:
  0.0 134.1 jit_solution(11012586094717859044)
XLA Ops:
  0.6 0.0 copy-start.1
  0.6 0.7 copy-done.1
  1.3 0.7 add_bitcast_fusion
  2.0 0.6 pad.4.meta
  2.6 128.8 %shard_map.122 = (bf16[128,2048]{1,0:T(8,128)(2,1)}, bf16[128,2048]{1,0:T(8,128)(2,1)}) custom-call(bf16[128,2048]{1,0:T(8,128)(2,1)} %hid.1, f32[1,2048]{1,0:T(1,128)} %bitcast.3, bf16[2,512,384]{2,1,0:T(8,128)(2,1)} %wg_in.1, bf16[2,512,384]{2,1,0:T(8,128)(2,1)} %wu_in.1, bf16[2,384,512]{2,1,0:T(8,128)(2,1)} %wd_in.1, s32[8,128]{1,0:T(8,128)} %pad.4.meta, ...), custom_call_target="tpu_custom_call" | custom-call | tf_op jit(solution)/shard_map/pallas_call | solution.py:450
  131.4 0.0 copy-start
  131.4 1.9 %copy.15 = bf16[128,2048]{1,0:T(8,128)(2,1)} copy(bf16[128,2048]{1,0:T(8,128)(2,1)} %get-tuple-element.4) | data formatting | bytes 1048576
  133.3 0.0 copy-done
  133.4 0.8 copy.16
Async XLA Ops:
  0.6 0.7 copy-start.1
  131.4 2.0 %copy-start = (bf16[128,2048]{1,0:T(8,128)(2,1)S(1)}, bf16[128,2048]{1,0:T(8,128)(2,1)}, u32[]{:S(2)}) copy-start(bf16[128,2048]{1,0:T(8,128)(2,1)} %get-tuple-element.5) | copy-start | bytes 1572868
